TPU v7x, 32 devices: a whole 2x2x4 slice. The times are simulated.
32 devices in a mesh: grp: 8 (over z, y), fsdp: 4 (over x, core).
Axes of the slice: x: 2, y: 2, z: 4, core: 2. Of those that a mesh axis runs over, the one named last changes fastest.
Arguments:
- layer_input: bfloat16 [2, 32768, 768], P(None, ('grp', 'fsdp')), may hold values from -6 to 6
- segment_ids: int32 [2, 32768], P(None, ('grp', 'fsdp')), may hold values from 0 to 255, never falling along the last dimension, each value on 1 to 1024 neighbouring positions
- bucket_table: int32 [2048], replicated, may hold values from 0 to 31, as said below
- gain_attn: bfloat16 [768], P('fsdp'), may hold values from 0.5 to 1.5
- weight_query: bfloat16 [768, 768], P('fsdp'), may hold values from -0.02734375 to 0.02734375
- weight_key: bfloat16 [768, 768], P('fsdp'), may hold values from -0.21875 to 0.21875
- weight_value: bfloat16 [768, 768], P('fsdp'), may hold values from -0.21875 to 0.21875
- weight_out: bfloat16 [768, 768], P('fsdp'), may hold values from -0.875 to 0.875
- gain_ffn: bfloat16 [768], P('fsdp'), may hold values from 0.5 to 1.5
- weight_in: bfloat16 [768, 3072], P('fsdp'), may hold values from -0.21875 to 0.21875
- weight_back: bfloat16 [3072, 768], P('fsdp'), may hold values from -0.109375 to 0.109375
- gain_final: bfloat16 [768], P('fsdp'), may hold values from 0.5 to 1.5
- weight_embed: bfloat16 [768, 128], P('fsdp'), may hold values from -0.21875 to 0.21875
- bias_table: bfloat16 [32, 12], P('fsdp'), may hold values from -4 to 4
- cotangent: bfloat16 [2, 32768, 128], P(None, ('grp', 'fsdp')), may hold values from -6 to 6
Outputs:
- states: float32 [2, 32768, 128], P(None, ('grp', 'fsdp'))
- grad_input: float32 [2, 32768, 768], P(None, ('grp', 'fsdp'))
- grad_gain_attn: float32 [768], P('fsdp')
- grad_query: float32 [768, 768], P('fsdp')
- grad_key: float32 [768, 768], P('fsdp')
- grad_value: float32 [768, 768], P('fsdp')
- grad_out: float32 [768, 768], P('fsdp')
- grad_gain_ffn: float32 [768], P('fsdp')
- grad_in: float32 [768, 3072], P('fsdp')
- grad_back: float32 [3072, 768], P('fsdp')
- grad_gain_final: float32 [768], P('fsdp')
- grad_embed: float32 [768, 128], P('fsdp')
- grad_table: float32 [32, 12], P('fsdp')
Inputs may be any that keep to these rules, and one draw needn't show every extreme that they name: `bucket_table`: entry 1024 + r is the bucket of a key r positions after its query (before it where r < 0); it is 0 for r = 0, below 16 for r <= 0, at least 16 for r > 0, and never falls as |r| grows on either side. `segment_ids`: along each micro-batch's row the ids never fall; a document spans 1 to 1024 positions and one spans exactly 1024.
All inputs are finite; a program needn't handle non-finite values.
Results may differ from a plain program's by a relative error of at most 0.018.
Values may be sent and summed in bfloat16 or wider, within the bound.
No kernel may reach another device: no remote copies, remote signals or barrier semaphores. Data moves between devices by JAX's collectives and lax.ppermute only.
A program may use at most 384 MiB of HBM per device.

v0:
```python
import jax
import jax.numpy as jnp
from jax import lax
from jax.sharding import PartitionSpec as P

EPS = 1e-06
HIGH = lax.Precision.HIGHEST
NEGATIVE = -1e30
ROOT_HALF = 0.7071067811865476
INV_ROOT_TWO_PI = 0.3989422804014327


def forward_dot(value, weight):
    return jnp.dot(value, weight, preferred_element_type=jnp.float32)


def outer(left, right):
    return lax.dot_general(
        left, right, (((0,), (0,)), ((), ())), preferred_element_type=jnp.float32
    )


def backward_dot(grad, weight):
    return lax.dot_general(
        grad, weight, (((1,), (1,)), ((), ())), preferred_element_type=jnp.float32
    )


def norm_scale(value):
    return lax.rsqrt(jnp.mean(value * value, axis=-1, keepdims=True) + EPS)


def norm_back(grad, value, scale, gain):
    weighted = grad * gain
    inner = jnp.mean(weighted * value, axis=-1, keepdims=True)
    dvalue = scale * weighted - value * (scale * scale * scale) * inner
    dgain = jnp.sum(grad * value * scale, axis=0)
    return (dvalue, dgain)


def gelu_slope(value):
    cdf = 0.5 * (1.0 + lax.erf(value * ROOT_HALF))
    return cdf + value * jnp.exp(-0.5 * value * value) * INV_ROOT_TWO_PI


def skew_bias(bias_rows, start, block):
    heads, twice = bias_rows.shape
    length = twice // 2
    ahead = lax.dynamic_slice_in_dim(bias_rows, length - start, length, 1)
    behind = lax.dynamic_slice_in_dim(bias_rows, length - start - block, block, 1)
    window = jnp.concatenate([ahead, behind], axis=1)
    period = length + block
    tiled = jnp.broadcast_to(window[:, None, :], (heads, block, period)).reshape(
        heads, block * period
    )
    skewed = tiled[:, : block * (period - 1)].reshape(heads, block, period - 1)
    return skewed[:, :, :length]


def block_scores(query_block, keys, bias_rows, start, segments, block):
    bias = skew_bias(bias_rows, start, block)
    scores = (
        jnp.einsum("qhd,khd->hqk", query_block, keys, preferred_element_type=jnp.float32) + bias
    )
    seg_rows = lax.dynamic_slice_in_dim(segments, start, block, 0)
    same = seg_rows[:, None] == segments[None, :]
    return jnp.where(same[None], scores, NEGATIVE)


def offset_sums(grad, start, table_pad):
    heads, block, length = grad.shape
    padded = jnp.pad(grad, ((0, 0), (0, 0), (block, 0)))
    flat = jnp.pad(padded.reshape(heads, block * (length + block)), ((0, 0), (0, block)))
    skewed = flat.reshape(heads, block, length + block + 1)
    column = jnp.sum(skewed, axis=1, dtype=jnp.float32)
    table_rows = lax.dynamic_slice_in_dim(table_pad, length - block - start, length + block + 1, 0)
    return jnp.dot(column, table_rows, precision=HIGH)


def body(
    layer_input,
    segment_ids,
    bucket_table,
    gain_attn,
    weight_query,
    weight_key,
    weight_value,
    weight_out,
    gain_ffn,
    weight_in,
    weight_back,
    gain_final,
    weight_embed,
    bias_table,
    cotangent,
):
    shards = (
        gain_attn,
        weight_query,
        weight_key,
        weight_value,
        weight_out,
        gain_ffn,
        weight_in,
        weight_back,
        gain_final,
        weight_embed,
        bias_table,
    )
    micro, seq, width = layer_input.shape
    heads = bias_table.shape[1]
    buckets = bias_table.shape[0] * lax.axis_size("fsdp")
    block = min(512, seq)
    starts = lax.iota(jnp.int32, seq // block) * block
    onehot = (bucket_table[:, None] == lax.iota(jnp.int32, buckets)[None, :]).astype(jnp.float32)
    table_pad = jnp.pad(onehot, ((0, 1), (0, 0)))
    states_list = []
    dinput_list = []
    summed = ()
    for step in range(micro):
        whole = (
            lax.all_gather(shards[0], "fsdp", axis=0, tiled=True),
            lax.all_gather(shards[1], "fsdp", axis=0, tiled=True),
            lax.all_gather(shards[2], "fsdp", axis=0, tiled=True),
            lax.all_gather(shards[3], "fsdp", axis=0, tiled=True),
            lax.all_gather(shards[4], "fsdp", axis=0, tiled=True),
            lax.all_gather(shards[5], "fsdp", axis=0, tiled=True),
            lax.all_gather(shards[6], "fsdp", axis=0, tiled=True),
            lax.all_gather(shards[7], "fsdp", axis=0, tiled=True),
            lax.all_gather(shards[8], "fsdp", axis=0, tiled=True),
            lax.all_gather(shards[9], "fsdp", axis=0, tiled=True),
            lax.all_gather(shards[10], "fsdp", axis=0, tiled=True),
        )
        g_one, wq, wk, wv, wo, g_two, wi, wb, g_three, we, table = whole
        xs = layer_input[step].astype(jnp.float32)
        segments = segment_ids[step]
        scale1 = norm_scale(xs)
        h1 = (xs * scale1 * g_one.astype(jnp.float32)).astype(jnp.bfloat16)
        query = forward_dot(h1, wq).astype(jnp.bfloat16).reshape(seq, heads, -1)
        keys = forward_dot(h1, wk).astype(jnp.bfloat16).reshape(seq, heads, -1)
        values = forward_dot(h1, wv).astype(jnp.bfloat16).reshape(seq, heads, -1)
        bias_rows = jnp.dot(onehot, table.astype(jnp.float32), precision=HIGH).T.astype(
            jnp.bfloat16
        )

        def attend(start):
            query_block = lax.dynamic_slice_in_dim(query, start, block, 0)
            scores = block_scores(query_block, keys, bias_rows, start, segments, block)
            top = jnp.max(scores, axis=-1, keepdims=True)
            expo = jnp.exp(scores - top)
            total = jnp.sum(expo, axis=-1, keepdims=True)
            probs = (expo / total).astype(jnp.bfloat16)
            result = jnp.einsum("hqk,khd->qhd", probs, values, preferred_element_type=jnp.float32)
            return (result, (top + jnp.log(total))[..., 0])

        blocks_out, log_sums = lax.map(attend, starts)
        attn = blocks_out.reshape(seq, width).astype(jnp.bfloat16)
        x2 = xs + forward_dot(attn, wo)
        scale2 = norm_scale(x2)
        h2 = (x2 * scale2 * g_two.astype(jnp.float32)).astype(jnp.bfloat16)
        pre = forward_dot(h2, wi)
        hidden = jax.nn.gelu(pre, approximate=False).astype(jnp.bfloat16)
        x3 = x2 + forward_dot(hidden, wb)
        scale3 = norm_scale(x3)
        h3 = (x3 * scale3 * g_three.astype(jnp.float32)).astype(jnp.bfloat16)
        states_list.append(forward_dot(h3, we))
        again = (
            lax.all_gather(shards[0], "fsdp", axis=0, tiled=True),
            lax.all_gather(shards[1], "fsdp", axis=0, tiled=True),
            lax.all_gather(shards[2], "fsdp", axis=0, tiled=True),
            lax.all_gather(shards[3], "fsdp", axis=0, tiled=True),
            lax.all_gather(shards[4], "fsdp", axis=0, tiled=True),
            lax.all_gather(shards[5], "fsdp", axis=0, tiled=True),
            lax.all_gather(shards[6], "fsdp", axis=0, tiled=True),
            lax.all_gather(shards[7], "fsdp", axis=0, tiled=True),
            lax.all_gather(shards[8], "fsdp", axis=0, tiled=True),
            lax.all_gather(shards[9], "fsdp", axis=0, tiled=True),
            lax.all_gather(shards[10], "fsdp", axis=0, tiled=True),
        )
        g_one, wq, wk, wv, wo, g_two, wi, wb, g_three, we, table = again
        upstream = cotangent[step]
        d_embed = outer(h3, upstream)
        dx3, dg_three = norm_back(
            backward_dot(upstream, we), x3, scale3, g_three.astype(jnp.float32)
        )
        d_branch = dx3.astype(jnp.bfloat16)
        d_back = outer(hidden, d_branch)
        d_pre = (backward_dot(d_branch, wb) * gelu_slope(pre)).astype(jnp.bfloat16)
        d_in = outer(h2, d_pre)
        ffn_part, dg_two = norm_back(backward_dot(d_pre, wi), x2, scale2, g_two.astype(jnp.float32))
        dx2 = dx3 + ffn_part
        d_attn_out = dx2.astype(jnp.bfloat16)
        d_out = outer(attn, d_attn_out)
        d_attn = backward_dot(d_attn_out, wo).astype(jnp.bfloat16).reshape(seq, heads, -1)

        def block_back(carry, item):
            dkey, dvalue, rel = carry
            start, log_block = item
            query_block = lax.dynamic_slice_in_dim(query, start, block, 0)
            dout_block = lax.dynamic_slice_in_dim(d_attn, start, block, 0)
            scores = block_scores(query_block, keys, bias_rows, start, segments, block)
            probs = jnp.exp(scores - log_block[:, :, None])
            dprob = jnp.einsum(
                "qhd,khd->hqk", dout_block, values, preferred_element_type=jnp.float32
            )
            dscore = (probs * (dprob - jnp.sum(dprob * probs, axis=-1, keepdims=True))).astype(
                jnp.bfloat16
            )
            dq_block = jnp.einsum("hqk,khd->qhd", dscore, keys, preferred_element_type=jnp.float32)
            dkey = dkey + jnp.einsum(
                "hqk,qhd->khd", dscore, query_block, preferred_element_type=jnp.float32
            )
            dvalue = dvalue + jnp.einsum(
                "hqk,qhd->khd",
                probs.astype(jnp.bfloat16),
                dout_block,
                preferred_element_type=jnp.float32,
            )
            rel = rel + offset_sums(dscore, start, table_pad)
            return ((dkey, dvalue, rel), dq_block)

        zeros_kv = jnp.zeros(keys.shape, jnp.float32)
        init = (zeros_kv, zeros_kv, jnp.zeros((heads, buckets), jnp.float32))
        (dkey_sum, dvalue_sum, rel_sum), dq_blocks = lax.scan(block_back, init, (starts, log_sums))
        dq = dq_blocks.reshape(seq, width).astype(jnp.bfloat16)
        dk = dkey_sum.reshape(seq, width).astype(jnp.bfloat16)
        dv = dvalue_sum.reshape(seq, width).astype(jnp.bfloat16)
        d_query = outer(h1, dq)
        d_key = outer(h1, dk)
        d_value = outer(h1, dv)
        dh1 = backward_dot(dq, wq) + backward_dot(dk, wk) + backward_dot(dv, wv)
        attn_part, dg_one = norm_back(dh1, xs, scale1, g_one.astype(jnp.float32))
        dinput_list.append(dx2 + attn_part)
        grads = (
            dg_one,
            d_query,
            d_key,
            d_value,
            d_out,
            dg_two,
            d_in,
            d_back,
            dg_three,
            d_embed,
            rel_sum.T,
        )
        shares = (
            lax.psum_scatter(
                grads[0].astype(jnp.bfloat16), "fsdp", scatter_dimension=0, tiled=True
            ).astype(jnp.float32),
            lax.psum_scatter(
                grads[1].astype(jnp.bfloat16), "fsdp", scatter_dimension=0, tiled=True
            ).astype(jnp.float32),
            lax.psum_scatter(
                grads[2].astype(jnp.bfloat16), "fsdp", scatter_dimension=0, tiled=True
            ).astype(jnp.float32),
            lax.psum_scatter(
                grads[3].astype(jnp.bfloat16), "fsdp", scatter_dimension=0, tiled=True
            ).astype(jnp.float32),
            lax.psum_scatter(
                grads[4].astype(jnp.bfloat16), "fsdp", scatter_dimension=0, tiled=True
            ).astype(jnp.float32),
            lax.psum_scatter(
                grads[5].astype(jnp.bfloat16), "fsdp", scatter_dimension=0, tiled=True
            ).astype(jnp.float32),
            lax.psum_scatter(
                grads[6].astype(jnp.bfloat16), "fsdp", scatter_dimension=0, tiled=True
            ).astype(jnp.float32),
            lax.psum_scatter(
                grads[7].astype(jnp.bfloat16), "fsdp", scatter_dimension=0, tiled=True
            ).astype(jnp.float32),
            lax.psum_scatter(
                grads[8].astype(jnp.bfloat16), "fsdp", scatter_dimension=0, tiled=True
            ).astype(jnp.float32),
            lax.psum_scatter(
                grads[9].astype(jnp.bfloat16), "fsdp", scatter_dimension=0, tiled=True
            ).astype(jnp.float32),
            lax.psum_scatter(
                grads[10].astype(jnp.bfloat16), "fsdp", scatter_dimension=0, tiled=True
            ).astype(jnp.float32),
        )
        summed = shares if step == 0 else tuple((a + b for a, b in zip(summed, shares)))
    totals = lax.psum(summed, "grp")
    return (jnp.stack(states_list), jnp.stack(dinput_list)) + tuple(totals)


def solution(mesh):
    placed = (
        P(None, ("grp", "fsdp"), None),
        P(None, ("grp", "fsdp")),
        P(),
        P("fsdp"),
        P("fsdp", None),
        P("fsdp", None),
        P("fsdp", None),
        P("fsdp", None),
        P("fsdp"),
        P("fsdp", None),
        P("fsdp", None),
        P("fsdp"),
        P("fsdp", None),
        P("fsdp", None),
        P(None, ("grp", "fsdp"), None),
    )
    return jax.shard_map(
        body,
        mesh=mesh,
        in_specs=placed,
        out_specs=(
            P(None, ("grp", "fsdp"), None),
            P(None, ("grp", "fsdp"), None),
            P("fsdp"),
            P("fsdp", None),
            P("fsdp", None),
            P("fsdp", None),
            P("fsdp", None),
            P("fsdp"),
            P("fsdp", None),
            P("fsdp", None),
            P("fsdp"),
            P("fsdp", None),
            P("fsdp", None),
        ),
        check_vma=False,
    )
```

profile of v0, /device:TPU:0, one launch (start us, length us, event | category | flops | bytes accessed | tf_op | source)
XLA Modules:
  0.0 3727.3 jit_solution(16283517211012601330)
XLA Ops:
  73.3 449.7 %while.75 = (s32[]{:T(128)}, bf16[2,512,12,64]{1,3,2,0:T(8,128)(2,1)}, f32[2,12,512]{2,1,0:T(8,128)S(1)}, s32[2]{0:T(128)}, s32[1024]{0:T(1024)S(1)}, /*index=5*...) while((s32[]{:T(128)}, ...), condition=%wide.region_11.12_spmd, body=%wide.region_8.11_spmd.sunk | while | flops 1667827712 | bytes 308926880 | solution.py:156
  85.4 65.1 %copy.145 = bf16[2,8,512,1536]{3,1,2,0:T(8,128)(2,1)} copy(bf16[2,8,512,1536]{3,2,1,0:T(8,128)(2,1)S(1)} %bitcast.373) | data formatting | bytes 50331648 | tf_op jit(solution)/shard_map/while
  171.1 87.1 %reshape.640 = bf16[12,512,1535]{2,1,0:T(8,128)(2,1)} reshape(bf16[12,785920]{1,0:T(8,128)(2,1)} %slice.141) | data formatting | bytes 37724160 | tf_op jit(solution)/shard_map/while/body/eval_jaxpr/reshape | solution.py:56
  307.5 65.1 %copy.145 = bf16[2,8,512,1536]{3,1,2,0:T(8,128)(2,1)} copy(bf16[2,8,512,1536]{3,2,1,0:T(8,128)(2,1)S(1)} %bitcast.373) | data formatting | bytes 50331648 | tf_op jit(solution)/shard_map/while
  393.1 87.1 %reshape.640 = bf16[12,512,1535]{2,1,0:T(8,128)(2,1)} reshape(bf16[12,785920]{1,0:T(8,128)(2,1)} %slice.141) | data formatting | bytes 37724160 | tf_op jit(solution)/shard_map/while/body/eval_jaxpr/reshape | solution.py:56
  537.3 448.8 %while.74 = (s32[]{:T(128)}, bf16[2,512,12,64]{1,3,2,0:T(8,128)(2,1)}, f32[2,12,512]{2,1,0:T(8,128)S(1)}, s32[2]{0:T(128)}, s32[1024]{0:T(1024)S(1)}, /*index=5*...) while((s32[]{:T(128)}, ...), condition=%wide.region_4.5_spmd, body=%wide.region_1.4_spmd.sunk | while | flops 1667827712 | bytes 308926880 | solution.py:156
  549.4 65.1 %copy.144 = bf16[2,8,512,1536]{3,1,2,0:T(8,128)(2,1)} copy(bf16[2,8,512,1536]{3,2,1,0:T(8,128)(2,1)S(1)} %bitcast.374) | data formatting | bytes 50331648 | tf_op jit(solution)/shard_map/while
  634.9 87.1 %reshape.639 = bf16[12,512,1535]{2,1,0:T(8,128)(2,1)} reshape(bf16[12,785920]{1,0:T(8,128)(2,1)} %slice.140) | data formatting | bytes 37724160 | tf_op jit(solution)/shard_map/while/body/eval_jaxpr/reshape | solution.py:56
  771.4 65.1 %copy.144 = bf16[2,8,512,1536]{3,1,2,0:T(8,128)(2,1)} copy(bf16[2,8,512,1536]{3,2,1,0:T(8,128)(2,1)S(1)} %bitcast.374) | data formatting | bytes 50331648 | tf_op jit(solution)/shard_map/while
  856.9 87.1 %reshape.639 = bf16[12,512,1535]{2,1,0:T(8,128)(2,1)} reshape(bf16[12,785920]{1,0:T(8,128)(2,1)} %slice.140) | data formatting | bytes 37724160 | tf_op jit(solution)/shard_map/while/body/eval_jaxpr/reshape | solution.py:56
  1159.8 968.3 %while.77 = (s32[]{:T(128)}, f32[1024,12,64]{0,2,1:T(8,128)}, f32[1024,12,64]{0,2,1:T(8,128)}, f32[12,32]{1,0:T(8,128)}, bf16[2,512,12,64]{1,3,2,0:T(8,128)(2,1)...) while((s32[]{:T(128)}, f32[1024,12,64]{0,2,1:T(8,128)}, ...), condition=%wide.region_26.27_spmd.clone, body=%wide.region_23.26_spmd.clone.sunk | while | flops 4119135488 | bytes 793059968 | solution.py:224
  1173.9 65.1 %copy.148 = bf16[2,8,512,1536]{3,1,2,0:T(8,128)(2,1)} copy(bf16[2,8,512,1536]{3,2,1,0:T(8,128)(2,1)S(1)} %bitcast.377) | data formatting | bytes 50331648 | tf_op jit(solution)/shard_map/while
  1259.4 87.4 %reshape.643 = bf16[12,512,1535]{2,1,0:T(8,128)(2,1)} reshape(bf16[12,785920]{1,0:T(8,128)(2,1)} %slice.145) | data formatting | bytes 37724160 | tf_op jit(solution)/shard_map/while/body/eval_jaxpr/reshape | solution.py:56
  1440.6 65.1 %copy.149 = bf16[2,8,512,1536]{3,1,2,0:T(8,128)(2,1)} copy(bf16[2,8,512,1536]{3,2,1,0:T(8,128)(2,1)S(1)} %bitcast.375) | data formatting | bytes 50331648 | tf_op jit(solution)/shard_map/while
  1532.8 92.0 %reshape.644 = f32[12,512,1537]{2,1,0:T(8,128)} reshape(f32[12,786944]{1,0:T(8,128)} %pad_convert_fusion.6) | data formatting | bytes 75546624 | tf_op jit(solution)/shard_map/while/body/eval_jaxpr/convert_element_type | solution.py:75
  1655.2 65.1 %copy.148 = bf16[2,8,512,1536]{3,1,2,0:T(8,128)(2,1)} copy(bf16[2,8,512,1536]{3,2,1,0:T(8,128)(2,1)S(1)} %bitcast.377) | data formatting | bytes 50331648 | tf_op jit(solution)/shard_map/while
  1740.8 87.4 %reshape.643 = bf16[12,512,1535]{2,1,0:T(8,128)(2,1)} reshape(bf16[12,785920]{1,0:T(8,128)(2,1)} %slice.145) | data formatting | bytes 37724160 | tf_op jit(solution)/shard_map/while/body/eval_jaxpr/reshape | solution.py:56
  1923.6 65.1 %copy.149 = bf16[2,8,512,1536]{3,1,2,0:T(8,128)(2,1)} copy(bf16[2,8,512,1536]{3,2,1,0:T(8,128)(2,1)S(1)} %bitcast.375) | data formatting | bytes 50331648 | tf_op jit(solution)/shard_map/while
  2015.8 92.0 %reshape.644 = f32[12,512,1537]{2,1,0:T(8,128)} reshape(f32[12,786944]{1,0:T(8,128)} %pad_convert_fusion.6) | data formatting | bytes 75546624 | tf_op jit(solution)/shard_map/while/body/eval_jaxpr/convert_element_type | solution.py:75
  2140.6 972.1 %while.76 = (s32[]{:T(128)}, f32[1024,12,64]{0,2,1:T(8,128)}, f32[1024,12,64]{0,2,1:T(8,128)}, f32[12,32]{1,0:T(8,128)}, bf16[2,512,12,64]{1,3,2,0:T(8,128)(2,1)...) while((s32[]{:T(128)}, f32[1024,12,64]{0,2,1:T(8,128)}, ...), condition=%wide.region_19.20_spmd.clone, body=%wide.region_16.19_spmd.clone.sunk | while | flops 4119135488 | bytes 793076352 | solution.py:224
  2154.6 65.1 %copy.146 = bf16[2,8,512,1536]{3,1,2,0:T(8,128)(2,1)} copy(bf16[2,8,512,1536]{3,2,1,0:T(8,128)(2,1)S(1)} %bitcast.378) | data formatting | bytes 50331648 | tf_op jit(solution)/shard_map/while
  2240.2 87.2 %reshape.641 = bf16[12,512,1535]{2,1,0:T(8,128)(2,1)} reshape(bf16[12,785920]{1,0:T(8,128)(2,1)} %slice.143) | data formatting | bytes 37724160 | tf_op jit(solution)/shard_map/while/body/eval_jaxpr/reshape | solution.py:56
  2421.2 65.1 %copy.147 = bf16[2,8,512,1536]{3,1,2,0:T(8,128)(2,1)} copy(bf16[2,8,512,1536]{3,2,1,0:T(8,128)(2,1)S(1)} %bitcast.376) | data formatting | bytes 50331648 | tf_op jit(solution)/shard_map/while
  2513.4 92.0 %reshape.642 = f32[12,512,1537]{2,1,0:T(8,128)} reshape(f32[12,786944]{1,0:T(8,128)} %pad_convert_fusion.5) | data formatting | bytes 75546624 | tf_op jit(solution)/shard_map/while/body/eval_jaxpr/convert_element_type | solution.py:75
  2635.8 65.1 %copy.146 = bf16[2,8,512,1536]{3,1,2,0:T(8,128)(2,1)} copy(bf16[2,8,512,1536]{3,2,1,0:T(8,128)(2,1)S(1)} %bitcast.378) | data formatting | bytes 50331648 | tf_op jit(solution)/shard_map/while
  2721.4 87.2 %reshape.641 = bf16[12,512,1535]{2,1,0:T(8,128)(2,1)} reshape(bf16[12,785920]{1,0:T(8,128)(2,1)} %slice.143) | data formatting | bytes 37724160 | tf_op jit(solution)/shard_map/while/body/eval_jaxpr/reshape | solution.py:56
  2904.1 65.1 %copy.147 = bf16[2,8,512,1536]{3,1,2,0:T(8,128)(2,1)} copy(bf16[2,8,512,1536]{3,2,1,0:T(8,128)(2,1)S(1)} %bitcast.376) | data formatting | bytes 50331648 | tf_op jit(solution)/shard_map/while
  2996.2 92.0 %reshape.642 = f32[12,512,1537]{2,1,0:T(8,128)} reshape(f32[12,786944]{1,0:T(8,128)} %pad_convert_fusion.5) | data formatting | bytes 75546624 | tf_op jit(solution)/shard_map/while/body/eval_jaxpr/convert_element_type | solution.py:75
  3261.5 48.3 %reduce-scatter.35.cloned.1.call-done = bf16[768,768]{1,0:T(8,128)(2,1)} async-done(((bf16[3072,768]{1,0:T(8,128)(2,1)}), bf16[768,768]{1,0:T(8,128)(2,1)}) %reduce-scatter.35.cloned.1.call-update) | async-done | bytes 1179664 | tf_op jit(solution)/shard_map/reduce_scatter | solution.py:269
  3309.8 50.4 %reduce-scatter.37.cloned.1.call-done = bf16[768,768]{1,0:T(8,128)(2,1)} async-done(((bf16[3072,768]{1,0:T(8,128)(2,1)}), bf16[768,768]{1,0:T(8,128)(2,1)}) %reduce-scatter.37.cloned.1.call-update) | async-done | bytes 1179664 | tf_op jit(solution)/shard_map/reduce_scatter | solution.py:269
  3410.6 51.0 %reduce-scatter.33.cloned.1.call-done = bf16[192,3072]{1,0:T(8,128)(2,1)} async-done(((bf16[768,3072]{1,0:T(8,128)(2,1)}), bf16[192,3072]{1,0:T(8,128)(2,1)}) %reduce-scatter.33.cloned.1.call-update) | async-done | bytes 1179664 | tf_op jit(solution)/shard_map/reduce_scatter | solution.py:266
  3529.6 180.4 %all-reduce.22.cloned.1.call-done = (f32[192,768]{1,0:T(8,128)}, f32[192,768]{1,0:T(8,128)}, f32[192,768]{1,0:T(8,128)}, f32[192,768]{1,0:T(8,128)}, f32[192,307...) async-done(((f32[192,768]{1,0:T(8,128)}, f32[192,768]{1,0:T(8,128)}, f32[192,768]{1,0:T(8,128)}, f32[192,768]{1,0:T(8,128)}, f32[192,3072]{1,0:T(8,128)}, ...) | async-done | bytes 7176208 | tf_op jit(solution)/shard_map/psum | solution.py:283
  (648 shorter events, 1468.6 us)
Async XLA Ops:
  7.3 39.9 %all-gather.9.cloned.1.call-start = ((), (), s32[]{:S(2)}) async-start(), calls=%async_computation.15 | async-start | bytes 1474560 | tf_op jit(solution)/shard_map/all_gather | solution.py:124
  8.0 43.1 %all-gather.11.cloned.1.call-start = ((), (), s32[]{:S(2)}) async-start(), calls=%async_computation.16 | async-start | bytes 1474560 | tf_op jit(solution)/shard_map/all_gather | solution.py:125
  8.7 59.3 %all-gather.7.cloned.1.call-start = ((), (), s32[]{:S(2)}) async-start(), calls=%async_computation.14 | async-start | bytes 1474560 | tf_op jit(solution)/shard_map/all_gather | solution.py:123
  9.5 980.2 %all-gather.13.cloned.1.call-start = ((), (), s32[]{:S(2)}) async-start(), calls=%async_computation.17 | async-start | bytes 1474560 | tf_op jit(solution)/shard_map/all_gather | solution.py:126
  10.0 987.6 %all-gather.15.cloned.1.call-start = ((), (), s32[]{:S(2)}) async-start(), calls=%async_computation.18 | async-start | bytes 5898240 | tf_op jit(solution)/shard_map/all_gather | solution.py:128
  10.6 1023.1 %all-gather.17.cloned.1.call-start = ((), (), s32[]{:S(2)}) async-start(), calls=%async_computation.19 | async-start | bytes 5898240 | tf_op jit(solution)/shard_map/all_gather | solution.py:129
  11.2 3185.8 %reduce-scatter.39.cloned.1.call-start = ((), (), s32[]{:S(2)}) async-start(), calls=%async_computation.32 | async-start | bytes 245760 | tf_op jit(solution)/shard_map/reduce_scatter | solution.py:275
  393.1 87.1 %copy-start.4 = (bf16[1024,12,64]{0,2,1:T(8,128)(2,1)S(1)}, bf16[1024,12,64]{0,2,1:T(8,128)(2,1)}, u32[]{:S(2)}) copy-start(bf16[1024,12,64]{0,2,1:T(8,128)(2,1)} %get-tuple-element.1776) | copy-start | bytes 4718596 | tf_op jit(solution)/shard_map/while
  856.9 87.1 %copy-start.2 = (bf16[1024,12,64]{0,2,1:T(8,128)(2,1)S(1)}, bf16[1024,12,64]{0,2,1:T(8,128)(2,1)}, u32[]{:S(2)}) copy-start(bf16[1024,12,64]{0,2,1:T(8,128)(2,1)} %get-tuple-element.1725) | copy-start | bytes 4718596 | tf_op jit(solution)/shard_map/while
  995.3 141.6 %copy-start.103 = (f32[1024]{0:T(1024)}, f32[1024]{0:T(1024)S(1)}, u32[]{:S(2)}) copy-start(f32[1024]{0:T(1024)S(1)} %get-tuple-element.1330) | copy-start | bytes 12292
  1093.3 2103.7 %reduce-scatter.41.cloned.1.call-start = ((), (), s32[]{:S(2)}) async-start(), calls=%async_computation.33 | async-start | bytes 245760 | tf_op jit(solution)/shard_map/reduce_scatter | solution.py:275
  1136.9 2061.6 %reduce-scatter.27.cloned.1.call-start = ((), (), s32[]{:S(2)}) async-start(), calls=%async_computation.26 | async-start | bytes 1474560 | tf_op jit(solution)/shard_map/reduce_scatter | solution.py:260
  1149.1 2049.4 %reduce-scatter.29.cloned.1.call-start = ((), (), s32[]{:S(2)}) async-start(), calls=%async_computation.27 | async-start | bytes 1474560 | tf_op jit(solution)/shard_map/reduce_scatter | solution.py:260
  1154.6 2045.8 %reduce-scatter.17.cloned.1.call-start = ((), (), s32[]{:S(2)}) async-start(), calls=%async_computation.21 | async-start | bytes 1474560 | tf_op jit(solution)/shard_map/reduce_scatter | solution.py:251
  1259.4 87.4 %copy-start.5 = (bf16[1024,12,64]{0,2,1:T(8,128)(2,1)S(1)}, bf16[1024,12,64]{0,2,1:T(8,128)(2,1)}, u32[]{:S(2)}) copy-start(bf16[1024,12,64]{0,2,1:T(8,128)(2,1)} %get-tuple-element.1843) | copy-start | bytes 4718596 | tf_op jit(solution)/shard_map/while
  1259.4 87.4 %copy-start.14 = (bf16[1024,12,64]{0,2,1:T(8,128)(2,1)S(1)}, bf16[1024,12,64]{0,2,1:T(8,128)(2,1)}, u32[]{:S(2)}) copy-start(bf16[1024,12,64]{0,2,1:T(8,128)(2,1)} %get-tuple-element.1840) | copy-start | bytes 4718596 | tf_op jit(solution)/shard_map/while
  1740.8 87.4 %copy-start.5 = (bf16[1024,12,64]{0,2,1:T(8,128)(2,1)S(1)}, bf16[1024,12,64]{0,2,1:T(8,128)(2,1)}, u32[]{:S(2)}) copy-start(bf16[1024,12,64]{0,2,1:T(8,128)(2,1)} %get-tuple-element.1843) | copy-start | bytes 4718596 | tf_op jit(solution)/shard_map/while
  1740.8 87.4 %copy-start.14 = (bf16[1024,12,64]{0,2,1:T(8,128)(2,1)S(1)}, bf16[1024,12,64]{0,2,1:T(8,128)(2,1)}, u32[]{:S(2)}) copy-start(bf16[1024,12,64]{0,2,1:T(8,128)(2,1)} %get-tuple-element.1840) | copy-start | bytes 4718596 | tf_op jit(solution)/shard_map/while
  2135.4 1065.0 %reduce-scatter.15.cloned.1.call-start = ((), (), s32[]{:S(2)}) async-start(), calls=%async_computation.20 | async-start | bytes 1474560 | tf_op jit(solution)/shard_map/reduce_scatter | solution.py:251
  2240.2 87.2 %copy-start.3 = (bf16[1024,12,64]{0,2,1:T(8,128)(2,1)S(1)}, bf16[1024,12,64]{0,2,1:T(8,128)(2,1)}, u32[]{:S(2)}) copy-start(bf16[1024,12,64]{0,2,1:T(8,128)(2,1)} %get-tuple-element.1915) | copy-start | bytes 4718596 | tf_op jit(solution)/shard_map/while
  2240.2 87.2 %copy-start.12 = (bf16[1024,12,64]{0,2,1:T(8,128)(2,1)S(1)}, bf16[1024,12,64]{0,2,1:T(8,128)(2,1)}, u32[]{:S(2)}) copy-start(bf16[1024,12,64]{0,2,1:T(8,128)(2,1)} %get-tuple-element.1912) | copy-start | bytes 4718596 | tf_op jit(solution)/shard_map/while
  2721.3 87.2 %copy-start.3 = (bf16[1024,12,64]{0,2,1:T(8,128)(2,1)S(1)}, bf16[1024,12,64]{0,2,1:T(8,128)(2,1)}, u32[]{:S(2)}) copy-start(bf16[1024,12,64]{0,2,1:T(8,128)(2,1)} %get-tuple-element.1915) | copy-start | bytes 4718596 | tf_op jit(solution)/shard_map/while
  2721.4 87.2 %copy-start.12 = (bf16[1024,12,64]{0,2,1:T(8,128)(2,1)S(1)}, bf16[1024,12,64]{0,2,1:T(8,128)(2,1)}, u32[]{:S(2)}) copy-start(bf16[1024,12,64]{0,2,1:T(8,128)(2,1)} %get-tuple-element.1912) | copy-start | bytes 4718596 | tf_op jit(solution)/shard_map/while
  3119.9 82.4 %reduce-scatter.21.cloned.1.call-start = ((), (), s32[]{:S(2)}) async-start(), calls=%async_computation.23 | async-start | bytes 1474560 | tf_op jit(solution)/shard_map/reduce_scatter | solution.py:254
  3125.9 77.2 %reduce-scatter.19.cloned.1.call-start = ((), (), s32[]{:S(2)}) async-start(), calls=%async_computation.22 | async-start | bytes 1474560 | tf_op jit(solution)/shard_map/reduce_scatter | solution.py:254
  3132.0 99.3 %reduce-scatter.25.cloned.1.call-start = ((), (), s32[]{:S(2)}) async-start(), calls=%async_computation.25 | async-start | bytes 1474560 | tf_op jit(solution)/shard_map/reduce_scatter | solution.py:257
  3137.9 121.7 %reduce-scatter.23.cloned.1.call-start = ((), (), s32[]{:S(2)}) async-start(), calls=%async_computation.24 | async-start | bytes 1474560 | tf_op jit(solution)/shard_map/reduce_scatter | solution.py:257
  3143.8 166.0 %reduce-scatter.35.cloned.1.call-start = ((), (), s32[]{:S(2)}) async-start(), calls=%async_computation.30 | async-start | bytes 5898240 | tf_op jit(solution)/shard_map/reduce_scatter | solution.py:269
  3153.5 206.7 %reduce-scatter.37.cloned.1.call-start = ((), (), s32[]{:S(2)}) async-start(), calls=%async_computation.31 | async-start | bytes 5898240 | tf_op jit(solution)/shard_map/reduce_scatter | solution.py:269
  3176.4 234.2 %reduce-scatter.31.cloned.1.call-start = ((), (), s32[]{:S(2)}) async-start(), calls=%async_computation.28 | async-start | bytes 5898240 | tf_op jit(solution)/shard_map/reduce_scatter | solution.py:266
  3186.7 274.9 %reduce-scatter.33.cloned.1.call-start = ((), (), s32[]{:S(2)}) async-start(), calls=%async_computation.29 | async-start | bytes 5898240 | tf_op jit(solution)/shard_map/reduce_scatter | solution.py:266
  3196.9 513.1 %all-reduce.22.cloned.1.call-start = ((), (), s32[]{:S(2)}) async-start(), calls=%async_computation.34 | async-start | bytes 14352384 | tf_op jit(solution)/shard_map/psum | solution.py:283
  (150 other events, 1544.2 us)
Sparse Core Ops, SparseCore 0:
  9.6 20.2 all-gather.8
  31.5 17.4 all-gather.10
  50.6 17.4 all-gather.6
  69.5 17.4 all-gather.12
  88.4 37.4 all-gather.14
  127.3 37.4 all-gather.16
  1093.4 19.7 reduce-scatter.38
  1137.0 19.7 reduce-scatter.40
  1159.4 25.7 reduce-scatter.26
  1187.8 25.7 reduce-scatter.28
  2135.5 25.7 reduce-scatter.16
  3120.1 25.7 reduce-scatter.14
  3149.0 25.7 reduce-scatter.20
  3177.3 25.7 reduce-scatter.18
  3205.5 25.7 reduce-scatter.24
  3233.8 25.6 reduce-scatter.22
  3261.9 47.8 reduce-scatter.34
  3312.3 47.8 reduce-scatter.36
  3362.7 47.8 reduce-scatter.30
  3413.7 47.8 reduce-scatter.32
  3468.3 241.7 all-reduce.21
where the time goes:
time: 3740 us; the launch traced here: 3730 us
  local copies, waits for them, and re-layouts  2170 us (58%)
  matrix products  621 us (17%)
  waiting for transfers between devices  450 us (12%)
  other arithmetic  355 us (9%)
  loops' own time  63.7 us (2%)
  blocking collectives  53.7 us (1%)
    while x140, local copies, waits for them, and re-layouts  818 us
    reshape x8, local copies, waits for them, and re-layouts, skew_bias(): skewed = tiled[:, :block * (period - 1)].reshape(heads, block, period - 1)  698 us
    convert_element_type x4, local copies, waits for them, and re-layouts, offset_sums(): column = jnp.sum(skewed, axis=1, dtype=jnp.float32)  368 us
    psum x1, waiting for transfers between devices, body(): totals = lax.psum(summed, 'grp')  180 us
    slice x8, local copies, waits for them, and re-layouts, skew_bias(): skewed = tiled[:, :block * (period - 1)].reshape(heads, block, period - 1)  163 us
    dot_general x8, matrix products, block_scores(): jnp.einsum('qhd,khd->hqk', query_block, keys, preferred_element_type=jnp....  128 us
    dot_general x14, matrix products, forward_dot(): return jnp.dot(value, weight, preferred_element_type=jnp.float32)  115 us
    convert_element_type x4, other arithmetic, offset_sums(): column = jnp.sum(skewed, axis=1, dtype=jnp.float32)  108 us
  transfers between devices with their start and end apart: 21, of which 9 were waited for; matrix products, arithmetic and copies ran while one was open for 82% of the time, Pallas kernels for 0%

commit v1 on v0

v1 whole, which is shorter than its diff:
```python
import functools
import jax, jax.numpy as jnp
from jax import lax
from jax.experimental import pallas as pl
from jax.experimental.pallas import tpu as pltpu
from jax.sharding import PartitionSpec as P

BQ = 256
STEP = 128
NEGATIVE = -1e30
VMEM_CAP = 60 * 1024 * 1024

NT = (((1,), (1,)), ((), ()))
NN = (((1,), (0,)), ((), ()))


def mm(a, b, dims=NN):
    return lax.dot_general(a, b, dims, preferred_element_type=jnp.float32)


def strip_kernel(rows_ref, strip_ref, *, length):
    rows = jnp.broadcast_to(rows_ref[0], (STEP, 2 * length))
    turned = pltpu.roll(rows, 2 * length - STEP, 1, stride=1, stride_axis=0)
    strip_ref[0] = turned[:, : 2 * length - STEP].T


def bias_strips(rows):
    heads, twice = rows.shape
    return pl.pallas_call(
        functools.partial(strip_kernel, length=twice // 2),
        grid=(heads,),
        in_specs=[pl.BlockSpec((1, 1, twice), lambda h: (h, 0, 0))],
        out_specs=pl.BlockSpec((1, twice - STEP, STEP), lambda h: (h, 0, 0)),
        out_shape=jax.ShapeDtypeStruct((heads, twice - STEP, STEP), jnp.float32),
        name="bias_strips",
        compiler_params=pltpu.CompilerParams(vmem_limit_bytes=VMEM_CAP),
    )(rows.reshape(heads, 1, twice))


def by_width(low_ref, width_ref, length, work):
    step = pl.program_id(0) * pl.num_programs(1) + pl.program_id(1)
    low = pl.multiple_of(low_ref[step], STEP)
    width = width_ref[step]
    for blocks in range(BQ // STEP, length // STEP + 1):

        @pl.when(width == blocks)
        def _(blocks=blocks):
            work(low, blocks * STEP)


def fwd_kernel(low_ref, width_ref, q_ref, k_ref, vt_ref, strip_ref, sk_ref, sq_ref,
               attn_ref, attnt_ref, prob_ref, inv_ref, mask_ref, *, heads, feat, length):
    start = pl.program_id(1) * BQ

    def work(low, width):
        keys = pl.ds(low, width)
        mask_ref[:width] = jnp.where(sk_ref[keys, :] == sq_ref[0], 0.0, NEGATIVE)
        row_a = pl.multiple_of(low - start + length - STEP, STEP)
        row_b = pl.multiple_of(low - start + length - 2 * STEP, STEP)

        def pair(index, carry):
            lanes = pl.ds(pl.multiple_of(index * 2 * feat, 2 * feat), 2 * feat)
            query = q_ref[:, lanes]
            key = k_ref[keys, lanes]
            left = lax.broadcasted_iota(jnp.int32, query.shape, 1) < feat
            outs = []
            for side in range(2):
                head = index * 2 + side
                own = jnp.where(left if side == 0 else ~left, query, jnp.zeros_like(query))
                bias = jnp.concatenate(
                    [strip_ref[head, pl.ds(row_a, width), :], strip_ref[head, pl.ds(row_b, width), :]],
                    axis=1,
                )
                scores = mm(key, own, NT) + bias + mask_ref[:width]
                top = jnp.max(scores, axis=0, keepdims=True)
                expo = jnp.exp(scores - top)
                inverse = 1.0 / jnp.sum(expo, axis=0, keepdims=True)
                prob = expo.astype(jnp.bfloat16)
                prob_ref[0, 0, head, keys, :] = prob
                value = vt_ref[pl.ds(pl.multiple_of(head * feat, feat), feat), keys]
                outs.append(mm(value, prob) * inverse)
                inv_ref[pl.ds(head, 1), :] = inverse
            both = jnp.concatenate(outs, axis=0)
            attnt_ref[pl.ds(pl.multiple_of(index * 2 * feat, 2 * feat), 2 * feat), :] = both.astype(jnp.bfloat16)
            attn_ref[:, lanes] = both.T.astype(jnp.bfloat16)
            return carry

        lax.fori_loop(0, heads // 2, pair, 0)

    by_width(low_ref, width_ref, length, work)


def attention(low, width, q, k, vt, strips, sk, sq, length):
    rows, model = q.shape
    heads = strips.shape[0]
    feat = model // heads
    seqs, blocks = rows // length, length // BQ
    at = lambda s, b, *_: (s * blocks + b, 0)
    whole = lambda s, b, *_: (s, 0)
    at_t = lambda s, b, *_: (0, s * blocks + b)
    spec = pltpu.PrefetchScalarGridSpec(
        num_scalar_prefetch=2,
        grid=(seqs, blocks),
        in_specs=[
            pl.BlockSpec((BQ, model), at),
            pl.BlockSpec((length, model), whole),
            pl.BlockSpec((model, length), lambda s, b, *_: (0, s)),
            pl.BlockSpec(strips.shape, lambda s, b, *_: (0, 0, 0), pipeline_mode=pl.Buffered(1)),
            pl.BlockSpec((length, 1), whole),
            pl.BlockSpec((1, 1, BQ), lambda s, b, *_: (s * blocks + b, 0, 0)),
        ],
        out_specs=[
            pl.BlockSpec((BQ, model), at),
            pl.BlockSpec((model, BQ), at_t),
            pl.BlockSpec((1, 1, heads, length, BQ), lambda s, b, *_: (s, b, 0, 0, 0)),
            pl.BlockSpec((heads, BQ), at_t),
        ],
        scratch_shapes=[pltpu.VMEM((length, BQ), jnp.float32)],
    )
    return pl.pallas_call(
        functools.partial(fwd_kernel, heads=heads, feat=feat, length=length),
        grid_spec=spec,
        out_shape=[
            jax.ShapeDtypeStruct((rows, model), jnp.bfloat16),
            jax.ShapeDtypeStruct((model, rows), jnp.bfloat16),
            jax.ShapeDtypeStruct((seqs, blocks, heads, length, BQ), jnp.bfloat16),
            jax.ShapeDtypeStruct((heads, rows), jnp.float32),
        ],
        name="attend",
        compiler_params=pltpu.CompilerParams(vmem_limit_bytes=VMEM_CAP),
    )(low, width, q, k, vt, strips, sk, sq)


def bwd_kernel(low_ref, width_ref, q_ref, k_ref, kt_ref, v_ref, attnt_ref, dot_ref, prob_ref, inv_ref,
               dq_ref, dk_ref, dv_ref, diag_ref, dka_ref, dva_ref, *, heads, feat, length):
    seq, block = pl.program_id(0), pl.program_id(1)
    start = block * BQ

    @pl.when(jnp.logical_and(seq == 0, block == 0))
    def _():
        diag_ref[...] = jnp.zeros_like(diag_ref)

    @pl.when(block == 0)
    def _():
        dka_ref[...] = jnp.zeros_like(dka_ref)
        dva_ref[...] = jnp.zeros_like(dva_ref)

    def work(low, width):
        keys = pl.ds(low, width)
        row_b = pl.multiple_of(low - start + length - 2 * STEP, STEP)

        def pair(index, carry):
            lanes = pl.ds(pl.multiple_of(index * 2 * feat, 2 * feat), 2 * feat)
            query = q_ref[:, lanes]
            value = v_ref[keys, lanes]
            left = lax.broadcasted_iota(jnp.int32, query.shape, 1) < feat
            dqs = []
            dkey = dval = None
            for side in range(2):
                head = index * 2 + side
                feats = pl.ds(pl.multiple_of(head * feat, feat), feat)
                own = jnp.where(left if side == 0 else ~left, query, jnp.zeros_like(query))
                inverse = inv_ref[pl.ds(head, 1), :]
                scaled = dot_ref[feats, :].astype(jnp.float32) * inverse
                delta = jnp.sum(scaled * attnt_ref[feats, :].astype(jnp.float32), axis=0, keepdims=True)
                scaled = scaled.astype(jnp.bfloat16)
                blank = jnp.zeros_like(scaled)
                padded = jnp.concatenate([scaled, blank] if side == 0 else [blank, scaled], axis=0)
                prob = prob_ref[0, 0, head, keys, :]
                dprob = mm(value, padded)
                dsf = prob.astype(jnp.float32) * (dprob - delta)
                ds = dsf.astype(jnp.bfloat16)
                dv_part = mm(prob, padded, NT)
                dk_part = mm(ds, own)
                dval = dv_part if dval is None else dval + dv_part
                dkey = dk_part if dkey is None else dkey + dk_part
                dqs.append(mm(kt_ref[feats, keys], ds))
                gap = jnp.zeros((STEP, STEP), jnp.float32)
                diag_ref[head, pl.ds(row_b, width + STEP), :] += (
                    jnp.concatenate([gap, dsf[:, :STEP]], axis=0)
                    + jnp.concatenate([dsf[:, STEP:], gap], axis=0)
                )
            dka_ref[keys, lanes] += dkey
            dva_ref[keys, lanes] += dval
            dq_ref[:, lanes] = jnp.concatenate(dqs, axis=0).T.astype(jnp.bfloat16)
            return carry

        lax.fori_loop(0, heads // 2, pair, 0)

    by_width(low_ref, width_ref, length, work)

    @pl.when(block == pl.num_programs(1) - 1)
    def _():
        dk_ref[...] = dka_ref[...].astype(jnp.bfloat16)
        dv_ref[...] = dva_ref[...].astype(jnp.bfloat16)


def attention_back(low, width, q, k, kt, v, attnt, dot, prob, inv, length):
    rows, model = q.shape
    heads = inv.shape[0]
    feat = model // heads
    seqs, blocks = rows // length, length // BQ
    at = lambda s, b, *_: (s * blocks + b, 0)
    whole = lambda s, b, *_: (s, 0)
    at_t = lambda s, b, *_: (0, s * blocks + b)
    strip = (heads, 2 * length - STEP, STEP)
    spec = pltpu.PrefetchScalarGridSpec(
        num_scalar_prefetch=2,
        grid=(seqs, blocks),
        in_specs=[
            pl.BlockSpec((BQ, model), at),
            pl.BlockSpec((length, model), whole),
            pl.BlockSpec((model, length), lambda s, b, *_: (0, s)),
            pl.BlockSpec((length, model), whole),
            pl.BlockSpec((model, BQ), at_t),
            pl.BlockSpec((model, BQ), at_t),
            pl.BlockSpec((1, 1, heads, length, BQ), lambda s, b, *_: (s, b, 0, 0, 0)),
            pl.BlockSpec((heads, BQ), at_t),
        ],
        out_specs=[
            pl.BlockSpec((BQ, model), at),
            pl.BlockSpec((length, model), whole),
            pl.BlockSpec((length, model), whole),
            pl.BlockSpec(strip, lambda s, b, *_: (0, 0, 0)),
        ],
        scratch_shapes=[pltpu.VMEM((length, model), jnp.float32)] * 2,
    )
    return pl.pallas_call(
        functools.partial(bwd_kernel, heads=heads, feat=feat, length=length),
        grid_spec=spec,
        out_shape=[
            jax.ShapeDtypeStruct((rows, model), jnp.bfloat16),
            jax.ShapeDtypeStruct((rows, model), jnp.bfloat16),
            jax.ShapeDtypeStruct((rows, model), jnp.bfloat16),
            jax.ShapeDtypeStruct(strip, jnp.float32),
        ],
        name="attend_back",
        compiler_params=pltpu.CompilerParams(vmem_limit_bytes=VMEM_CAP),
    )(low, width, q, k, kt, v, attnt, dot, prob, inv)


def key_ranges(seg, length):
    firsts, lasts = seg[:, ::BQ], seg[:, BQ - 1 :: BQ]
    low = jnp.sum((seg[:, None, :] < firsts[:, :, None]).astype(jnp.int32), axis=-1)
    high = jnp.sum((seg[:, None, :] <= lasts[:, :, None]).astype(jnp.int32), axis=-1)
    low = low // STEP
    width = (high + STEP - 1) // STEP - low
    return (low * STEP).reshape(-1), width.reshape(-1)


def unskew_kernel(strip_ref, out_ref, *, length):
    data = strip_ref[0]
    data = jnp.concatenate([data, jnp.zeros((STEP, STEP), jnp.float32)], axis=0)
    rows = lax.broadcasted_iota(jnp.int32, (STEP, STEP), 0)
    cols = lax.broadcasted_iota(jnp.int32, (STEP, STEP), 1)
    flip = (rows + cols == STEP - 1).astype(jnp.bfloat16)
    high = data.astype(jnp.bfloat16)
    low = (data - high.astype(jnp.float32)).astype(jnp.bfloat16)
    turned = (mm(high, flip) + mm(low, flip)).T
    out_ref[0] = jnp.sum(pltpu.roll(turned, 1, 1, stride=1, stride_axis=0), axis=0, keepdims=True)


def diagonal_sums(strips):
    heads, rows, _ = strips.shape
    length = (rows + STEP) // 2
    out = pl.pallas_call(
        functools.partial(unskew_kernel, length=length),
        grid=(heads,),
        in_specs=[pl.BlockSpec((1, rows, STEP), lambda h: (h, 0, 0))],
        out_specs=pl.BlockSpec((1, 1, 2 * length), lambda h: (h, 0, 0)),
        out_shape=jax.ShapeDtypeStruct((heads, 1, 2 * length), jnp.float32),
        name="diagonal_sums",
        compiler_params=pltpu.CompilerParams(vmem_limit_bytes=VMEM_CAP),
    )(strips)
    return out.reshape(heads, 2 * length)


EPS = 1e-06
ROOT_HALF = 0.7071067811865476
INV_ROOT_TWO_PI = 0.3989422804014327
BF = jnp.bfloat16
F32 = jnp.float32


def bits_of(axis):
    size = lax.axis_size(axis)
    count = size.bit_length() - 1
    assert size == 1 << count
    return count


def swap(value, axis, bit):
    size = lax.axis_size(axis)
    return lax.ppermute(value, axis, [(i, i ^ (1 << bit)) for i in range(size)])


def collect(shard):
    me = lax.axis_index("fsdp")
    held = {0: shard}
    for bit in reversed(range(bits_of("fsdp"))):
        got = {k ^ (1 << bit): swap(v, "fsdp", bit) for k, v in held.items()}
        held.update(got)
    rows = shard.shape[0]
    whole = jnp.zeros((rows * len(held),) + shard.shape[1:], shard.dtype)
    for k, v in held.items():
        whole = lax.dynamic_update_slice_in_dim(whole, v, (me ^ k) * rows, 0)
    return whole


def share_out(grad):
    me = lax.axis_index("fsdp")
    size = lax.axis_size("fsdp")
    rows = grad.shape[0] // size
    part = {k: lax.dynamic_slice_in_dim(grad, (me ^ k) * rows, rows, 0) for k in range(size)}
    for bit in range(bits_of("fsdp")):
        step = 1 << bit
        kept = {}
        for k in part:
            if not k & step:
                kept[k] = part[k] + swap(part[k ^ step].astype(BF), "fsdp", bit).astype(F32)
        part = kept
    return part[0]


def halves(value, axis, side):
    size = value.shape[axis] // 2
    return (
        lax.dynamic_slice_in_dim(value, side * size, size, axis),
        lax.dynamic_slice_in_dim(value, (1 - side) * size, size, axis),
    )


def total(value):
    me = lax.axis_index("grp")
    count = bits_of("grp")
    trail = []
    for bit in range(count):
        axis = 1 if bit == 0 else 0
        side = (me >> bit) & 1
        mine, other = halves(value, axis, side)
        value = mine + swap(other.astype(BF), "grp", bit).astype(F32)
        trail.append((axis, side))
    value = value.astype(BF)
    for bit in reversed(range(count)):
        axis, side = trail[bit]
        other = swap(value, "grp", bit)
        value = jnp.where(
            side == 0,
            jnp.concatenate([value, other], axis=axis),
            jnp.concatenate([other, value], axis=axis),
        )
    return value.astype(F32)


def total_small(value):
    for axis in ("fsdp", "grp"):
        for bit in range(bits_of(axis)):
            value = value + swap(value, axis, bit)
    return value


def forward_dot(value, weight):
    return mm(value, weight)


def outer(left, right):
    return mm(left, right, (((0,), (0,)), ((), ())))


def backward_dot(grad, weight):
    return mm(grad, weight, NT)


def norm_scale(value):
    return lax.rsqrt(jnp.mean(value * value, axis=-1, keepdims=True) + EPS)


def norm_back(grad, value, scale, gain):
    weighted = grad * gain
    inner = jnp.mean(weighted * value, axis=-1, keepdims=True)
    dvalue = scale * weighted - value * (scale * scale * scale) * inner
    dgain = jnp.sum(grad * value * scale, axis=0)
    return (dvalue, dgain)


def gelu_slope(value):
    cdf = 0.5 * (1.0 + lax.erf(value * ROOT_HALF))
    return cdf + value * jnp.exp(-0.5 * value * value) * INV_ROOT_TWO_PI


def body(
    layer_input,
    segment_ids,
    bucket_table,
    gain_attn,
    weight_query,
    weight_key,
    weight_value,
    weight_out,
    gain_ffn,
    weight_in,
    weight_back,
    gain_final,
    weight_embed,
    bias_table,
    cotangent,
):
    micro, length, width = layer_input.shape
    heads = bias_table.shape[1]
    size = lax.axis_size("fsdp")
    me = lax.axis_index("fsdp")
    buckets = bias_table.shape[0] * size
    rows = micro * length
    small = jnp.concatenate([gain_attn, gain_ffn, gain_final, bias_table.reshape(-1)]).reshape(1, -1)
    small = collect(small)
    part = width // size
    g_one = small[:, :part].reshape(width).astype(F32)
    g_two = small[:, part : 2 * part].reshape(width).astype(F32)
    g_three = small[:, 2 * part : 3 * part].reshape(width).astype(F32)
    table = small[:, 3 * part :].reshape(buckets, heads)
    wq, wk, wv = collect(weight_query), collect(weight_key), collect(weight_value)
    wo, wi, wb, we = collect(weight_out), collect(weight_in), collect(weight_back), collect(weight_embed)

    onehot = (bucket_table[:, None] == lax.iota(jnp.int32, buckets)[None, :]).astype(BF)
    bias_rows = lax.dot_general(table, onehot, (((0,), (1,)), ((), ())), preferred_element_type=F32)
    strips = bias_strips(bias_rows)
    low, wide = key_ranges(segment_ids, length)
    seg_col = segment_ids.reshape(rows, 1)
    seg_row = segment_ids.reshape(rows // BQ, 1, BQ)

    xs = layer_input.reshape(rows, width).astype(F32)
    scale1 = norm_scale(xs)
    h1 = (xs * scale1 * g_one).astype(BF)
    query, key, value = (forward_dot(h1, w).astype(BF) for w in (wq, wk, wv))
    key_t = mm(wk, h1, (((0,), (1,)), ((), ()))).astype(BF)
    value_t = mm(wv, h1, (((0,), (1,)), ((), ()))).astype(BF)
    attn, attn_t, probs, inverse = attention(
        low, wide, query, key, value_t, strips, seg_col, seg_row, length
    )
    x2 = xs + forward_dot(attn, wo)
    scale2 = norm_scale(x2)
    h2 = (x2 * scale2 * g_two).astype(BF)
    pre = forward_dot(h2, wi)
    hidden = jax.nn.gelu(pre, approximate=False).astype(BF)
    slope = gelu_slope(pre).astype(BF)
    x3 = x2 + forward_dot(hidden, wb)
    scale3 = norm_scale(x3)
    h3 = (x3 * scale3 * g_three).astype(BF)
    states = forward_dot(h3, we)

    upstream = cotangent.reshape(rows, -1)
    d_embed = outer(h3, upstream)
    dx3, dg_three = norm_back(backward_dot(upstream, we), x3, scale3, g_three)
    d_branch = dx3.astype(BF)
    d_back = outer(hidden, d_branch)
    d_pre = (backward_dot(d_branch, wb) * slope.astype(F32)).astype(BF)
    d_in = outer(h2, d_pre)
    ffn_part, dg_two = norm_back(backward_dot(d_pre, wi), x2, scale2, g_two)
    dx2 = dx3 + ffn_part
    d_attn_out = dx2.astype(BF)
    d_out = outer(attn, d_attn_out)
    d_attn_t = mm(wo, d_attn_out, NT).astype(BF)
    dq, dk, dv, diag = attention_back(
        low, wide, query, key, key_t, value, attn_t, d_attn_t, probs, inverse, length
    )
    d_query, d_key, d_value = outer(h1, dq), outer(h1, dk), outer(h1, dv)
    dh1 = backward_dot(dq, wq) + backward_dot(dk, wk) + backward_dot(dv, wv)
    attn_part, dg_one = norm_back(dh1, xs, scale1, g_one)
    d_input = dx2 + attn_part
    d_table = jnp.dot(
        diagonal_sums(diag), onehot.astype(F32), precision=lax.Precision.HIGHEST
    ).T

    g_embed, g_back, g_in, g_out, g_query, g_key, g_value = (
        total(share_out(g)) for g in (d_embed, d_back, d_in, d_out, d_query, d_key, d_value)
    )
    tiny = jnp.concatenate([dg_one, dg_two, dg_three, d_table.reshape(-1)]).reshape(-1, 128)
    tiny = total_small(tiny).reshape(-1)

    def own(vector, count):
        return lax.dynamic_slice_in_dim(vector, me * count, count, 0)

    gain_grads = [own(tiny[k * width : (k + 1) * width], part) for k in range(3)]
    g_table = own(tiny[3 * width :].reshape(buckets, heads), buckets // size)
    return (
        states.reshape(micro, length, -1),
        d_input.reshape(micro, length, width),
        gain_grads[0],
        g_query,
        g_key,
        g_value,
        g_out,
        gain_grads[1],
        g_in,
        g_back,
        gain_grads[2],
        g_embed,
        g_table,
    )


def solution(mesh):
    placed = (
        P(None, ("grp", "fsdp"), None),
        P(None, ("grp", "fsdp")),
        P(),
        P("fsdp"),
        P("fsdp", None),
        P("fsdp", None),
        P("fsdp", None),
        P("fsdp", None),
        P("fsdp"),
        P("fsdp", None),
        P("fsdp", None),
        P("fsdp"),
        P("fsdp", None),
        P("fsdp", None),
        P(None, ("grp", "fsdp"), None),
    )
    return jax.shard_map(
        body,
        mesh=mesh,
        in_specs=placed,
        out_specs=(
            P(None, ("grp", "fsdp"), None),
            P(None, ("grp", "fsdp"), None),
            P("fsdp"),
            P("fsdp", None),
            P("fsdp", None),
            P("fsdp", None),
            P("fsdp", None),
            P("fsdp"),
            P("fsdp", None),
            P("fsdp", None),
            P("fsdp"),
            P("fsdp", None),
            P("fsdp", None),
        ),
        check_vma=False,
    )
```

time: 3740 us -> 782 us (0.21)
  local copies, waits for them, and re-layouts: 2170 us -> 67.1 us
  matrix products: 621 us -> 234 us
  other arithmetic: 355 us -> 43.6 us
  waiting for transfers between devices: 450 us -> 155 us
  Pallas kernels: 0 us -> 139 us
  starting transfers between devices: 0.85 us -> 125 us
  loops' own time: 63.7 us -> 0 us
  blocking collectives: 53.7 us -> 0 us
    while x140 -> x0, local copies, waits for them, and re-layouts: 818 us -> none
    reshape x8 -> x7, local copies, waits for them, and re-layouts: 698 us -> 3.1 us  [the longest x1 1.31 us: body(): seg_row = segment_ids.reshape(rows // BQ, 1, BQ)]
    dot_general x75 -> x25, matrix products: 621 us -> 234 us  [the longest x23 232 us: mm(): return lax.dot_general(a, b, dims, preferred_element_type=jnp.float32)]
    convert_element_type x10 -> x31, local copies, waits for them, and re-layouts: 381 us -> 18.8 us  [the longest x7 17.4 us: share_out(): kept[k] = part[k] + swap(part[k ^ step].astype(BF), 'fsdp', bit).astype(F32)]
    reduce_scatter x14 -> x0, waiting for transfers between devices: 252 us -> none  [the longest x2 98.7 us: body(): lax.psum_scatter(grads[7].astype(jnp.bfloat16), 'fsdp', scatter_dimension...]
    convert_element_type x17 -> x23, other arithmetic: 203 us -> 19.4 us  [the longest x7 7.71 us: total(): return value.astype(F32)]
    psum x1 -> x0, waiting for transfers between devices: 180 us -> none  [body(): totals = lax.psum(summed, 'grp')]
    slice x10 -> x5, local copies, waits for them, and re-layouts: 167 us -> 1.65 us  [the longest x2 1.57 us: key_ranges(): firsts, lasts = (seg[:, ::BQ], seg[:, BQ - 1::BQ])]
  transfers between devices with their start and end apart: 21 -> 92, of which waited for: 9 -> 42; matrix products, arithmetic and copies ran while one was open for 82% -> 27% of each run, Pallas kernels for 0% -> 11%
where the time goes in v1:
time: 782 us; the launch traced here: 767 us
  matrix products  234 us (30%)
  waiting for transfers between devices  155 us (20%)
  Pallas kernels  139 us (18%)
  starting transfers between devices  125 us (16%)
  local copies, waits for them, and re-layouts  67.1 us (9%)
  other arithmetic  43.6 us (6%)
    dot_general x23, matrix products, mm(): return lax.dot_general(a, b, dims, preferred_element_type=jnp.float32)  232 us
    ppermute x92, waiting for transfers between devices, swap(): return lax.ppermute(value, axis, [(i, i ^ 1 << bit) for i in range(size)])  155 us
    ppermute x92, starting transfers between devices, swap(): return lax.ppermute(value, axis, [(i, i ^ 1 << bit) for i in range(size)])  125 us
    pallas_call x1, Pallas kernels, attention(): pl.pallas_call(functools.partial(fwd_kernel, heads=heads, feat=feat, leng...  60.1 us
    pallas_call x1, Pallas kernels, attention_back(): pl.pallas_call(functools.partial(bwd_kernel, heads=heads, feat=feat, leng...  52.5 us
    dynamic_update_slice x32, local copies, waits for them, and re-layouts, collect(): whole = lax.dynamic_update_slice_in_dim(whole, v, (me ^ k) * rows, 0)  31.7 us
    convert_element_type x7, local copies, waits for them, and re-layouts, share_out(): kept[k] = part[k] + swap(part[k ^ step].astype(BF), 'fsdp', bit).astype(F32)  17.4 us
    pallas_call x1, Pallas kernels, diagonal_sums(): pl.pallas_call(functools.partial(unskew_kernel, length=length), grid=(hea...  15.7 us
  transfers between devices with their start and end apart: 92, of which 42 were waited for; matrix products, arithmetic and copies ran while one was open for 27% of the time, Pallas kernels for 11%

profile of v1, /device:TPU:0, one launch (start us, length us, event | category | flops | bytes accessed | tf_op | source)
XLA Modules:
  0.0 767.4 jit_solution(8502462080894409835)
XLA Ops:
  40.8 11.0 %bias_strips.1.strip_ref = f32[12,1920,128]{2,1,0:T(8,128)} custom-call(f32[12,1,2048]{2,1,0:T(1,128)} %reshape.177.rows_ref), custom_call_target="tpu_custom_call" | custom-call | tf_op jit(solution)/shard_map/bias_strips/pallas_call | solution.py:29
  85.7 5.2 convolution_convert_fusion.5.q_ref
  90.9 60.1 %attend.1 = (bf16[2048,768]{1,0:T(8,128)(2,1)}, bf16[768,2048]{1,0:T(8,128)(2,1)}, bf16[2,4,12,1024,256]{4,3,2,1,0:T(8,128)(2,1)}, f32[12,2048]{1,0:T(8,128)}) custom-call(s32[8]{0:T(128)} %broadcast_multiply_fusion.3.low_ref, s32[8]{0:T(128)} %get-tuple-element.38.width_ref, bf16[2048,768]{1,0:T(8,128)(2,1)} %convolution_convert_fusion.5.q_ref, ...), custom_call_target="tpu_custom_call" | custom-call | tf_op jit(solution)/shard_map/attend/pallas_call | solution.py:120
  151.7 5.4 multiply_reduce_fusion.4
  165.6 7.6 collective-permute-start.17
  184.4 66.5 %fusion.2 = (bf16[2048,3072]{1,0:T(8,128)(2,1)}, f32[2048,3072]{1,0:T(8,128)}) fusion(bf16[768,3072]{1,0:T(8,128)(2,1)} %constant_dynamic-update-slice_fusion.8, f32[2048,768]{1,0:T(8,128)S(1)} %get-tuple-element.67, f32[768]{0:T(1024)S(1)} %reshape.189, f32[2048]{0:T(1024)S(1)} %get-tuple-element.60), kind=kOutput, calls=%fused_computation.4 | convolution fusion | flops 10077339648 | bytes 48770048 | tf_op jit(solution)/shard_map/dot_general | solution.py:18
  253.4 14.9 %multiply_reduce_fusion.3 = (f32[2048]{0:T(1024)S(1)}, f32[2048,768]{1,0:T(8,128)S(1)}) fusion(f32[2048,768]{1,0:T(8,128)S(1)} %get-tuple-element.67, bf16[2048,3072]{1,0:T(8,128)(2,1)} %get-tuple-element.68, bf16[3072,768]{1,0:T(8,128)(2,1)} %constant_dynamic-update-slice_fusion.4), kind=kOutput, calls=%fused_computation.52 | convolution fusion | flops 9668392960 | bytes 29892608 | tf_op jit(solution)/shard_map/dot_general | solution.py:18
  273.0 15.7 %fusion.29 = f32[3072,768]{1,0:T(8,128)} fusion(bf16[2048,3072]{1,0:T(8,128)(2,1)} %get-tuple-element.68, f32[2048,768]{1,0:T(8,128)S(1)} %get-tuple-element.44), kind=kOutput, calls=%fused_computation.73 | convolution fusion | flops 9665249280 | bytes 28311552 | tf_op jit(solution)/shard_map/dot_general | solution.py:18
  288.7 23.0 %multiply_convert_fusion = bf16[2048,3072]{1,0:T(8,128)(2,1)} fusion(bf16[3072,768]{1,0:T(8,128)(2,1)} %constant_dynamic-update-slice_fusion.4, f32[2048,3072]{1,0:T(8,128)} %get-tuple-element.69, f32[2048,768]{1,0:T(8,128)S(1)} %get-tuple-element.44), kind=kOutput, calls=%fused_computation.10 | convolution fusion | flops 9740746752 | bytes 48758784 | tf_op jit(solution)/shard_map/dot_general | solution.py:18
  311.7 15.7 %fusion.51 = f32[768,3072]{1,0:T(8,128)} fusion(bf16[2048,3072]{1,0:T(8,128)(2,1)} %multiply_convert_fusion, f32[2048,768]{1,0:T(8,128)S(1)} %bitcast.110, f32[768]{0:T(1024)S(1)} %reshape.189, f32[2048]{0:T(1024)S(1)} %get-tuple-element.60), kind=kOutput, calls=%fused_computation.237 | convolution fusion | flops 9668395008 | bytes 28322816 | tf_op jit(solution)/shard_map/dot_general | solution.py:18
  327.5 17.4 %multiply_reduce_fusion = (f32[768]{0:T(1024)S(1)}, f32[2048]{0:T(1024)S(1)}, f32[2048,768]{1,0:T(8,128)}) fusion(f32[2048,768]{1,0:T(8,128)} %copy-done.5, f32[2048]{0:T(1024)S(1)} %get-tuple-element.60, f32[768]{0:T(1024)S(1)} %reshape.189, bf16[2048,3072]{1,0:T(8,128)(2,1)} %multiply_convert_fusion, bf16[768,3072]{1,0:T(8,128)(2,1)} %constant_dynamic-update-slice_fusion.8), kind=kOutput, calls=%fused_computation.45 | convolution fusion | flops 9673110528 | bytes 29906944 | tf_op jit(solution)/shard_map/dot_general | solution.py:18
  344.9 6.0 subtract_add_fusion
  355.1 5.3 convolution_convert_fusion.dot_ref
  360.4 52.5 %attend_back.1 = (bf16[2048,768]{1,0:T(8,128)(2,1)}, bf16[2048,768]{1,0:T(8,128)(2,1)}, bf16[2048,768]{1,0:T(8,128)(2,1)}, f32[12,1920,128]{2,1,0:T(8,128)}) custom-call(s32[8]{0:T(128)} %broadcast_multiply_fusion.3.low_ref, s32[8]{0:T(128)} %get-tuple-element.38.width_ref, bf16[2048,768]{1,0:T(8,128)(2,1)} %convolution_convert_fusion.5.q_ref, ...), custom_call_target="tpu_custom_call" | custom-call | tf_op jit(solution)/shard_map/attend_back/pallas_call | solution.py:228
  413.0 7.1 fusion.57
  428.7 6.0 fusion.54
  438.3 6.8 collective-permute-start.84
  460.5 15.7 %diagonal_sums.1 = f32[12,1,2048]{2,1,0:T(1,128)} custom-call(f32[12,1920,128]{2,1,0:T(8,128)} %get-tuple-element.28.strip_ref), custom_call_target="tpu_custom_call" | custom-call | tf_op jit(solution)/shard_map/diagonal_sums/pallas_call | solution.py:266
  478.3 10.6 %fusion.25 = (f32[768]{0:T(1024)S(1)}, f32[2048]{0:T(1024)S(1)}, f32[2048,768]{1,0:T(8,128)S(1)}) fusion(bf16[2,1024,768]{2,1,0:T(8,128)(2,1)} %param.15, f32[2048]{0:T(1024)S(1)} %bitcast.116, f32[768]{0:T(1024)S(1)} %copy-done.32, f32[2048,768]{1,0:T(8,128)} %fusion.54, f32[2048,768]{1,0:T(8,128)} %fusion.55, bf16[2048,768]{1,0:T(8,128)(2,1)} %get-tuple-element.27, ...), kind=kOutput, calls=%fused_computation.44 | convolution fusion | flops 2430072064 | bytes 26368000 | tf_op jit(solution)/shard_map/dot_general | solution.py:18
  494.1 16.4 %collective-permute-start.85 = (bf16[192,128]{1,0:T(8,128)(2,1)S(1)}, bf16[192,128]{1,0:T(8,128)(2,1)S(1)}, u32[]{:S(2)}, u32[]{:S(2)}) collective-permute-start(bf16[192,128]{1,0:T(8,128)(2,1)S(1)} %add_convert_fusion.8), channel_id=1, source_target_pairs={{0,2},{1,3},{2,0},{3,1},{4,6},{5,7},{6,4},{7,5},{8,10},{9,11},{10,... | collective-permute-start | bytes 147464 | tf_op jit(solution)/shard_map/ppermute | solution.py:294
  512.8 16.8 %collective-permute-start.86 = (bf16[192,64]{1,0:T(8,128)(2,1)S(1)}, bf16[192,64]{1,0:T(8,128)(2,1)S(1)}, u32[]{:S(2)}, u32[]{:S(2)}) collective-permute-start(bf16[192,64]{1,0:T(8,128)(2,1)S(1)} %dynamic-slice_convert_fusion.26), channel_id=1, source_target_pairs={{0,4},{4,0},{8,12},{12,8},{16,20},{20,16},{24,28},{28,24},{1,5},{5... | collective-permute-start | bytes 73736 | tf_op jit(solution)/shard_map/ppermute | solution.py:294
  561.9 6.3 collective-permute-done.58
  632.9 5.0 collective-permute-done.52
  645.9 5.0 collective-permute-done.62
  651.0 4.8 collective-permute-done.53
  662.7 8.4 %collective-permute-done.76 = bf16[768,768]{1,0:T(8,128)(2,1)S(1)} collective-permute-done((bf16[768,768]{1,0:T(8,128)(2,1)S(1)}, bf16[768,768]{1,0:T(8,128)(2,1)S(1)}, u32[]{:S(2)}, u32[]{:S(2)}) %collective-permute-start.76) | collective-permute-done | bytes 1179680 | tf_op jit(solution)/shard_map/ppermute | solution.py:294
  675.3 8.4 %collective-permute-done.67 = bf16[192,3072]{1,0:T(8,128)(2,1)S(1)} collective-permute-done((bf16[192,3072]{1,0:T(8,128)(2,1)S(1)}, bf16[192,3072]{1,0:T(8,128)(2,1)S(1)}, u32[]{:S(2)}, u32[]{:S(2)}) %collective-permute-start.67) | collective-permute-done | bytes 1179680 | tf_op jit(solution)/shard_map/ppermute | solution.py:294
  687.8 5.8 collective-permute-done.77
  702.0 5.6 collective-permute-done.78
  710.3 6.8 collective-permute-done.69
  717.1 6.0 collective-permute-done.79
  724.0 5.4 collective-permute-done.70
  (450 shorter events, 311.6 us)
Async XLA Ops:
  0.7 56.2 %collective-permute-start.6 = (bf16[192,768]{1,0:T(8,128)(2,1)}, bf16[192,768]{1,0:T(8,128)(2,1)}, u32[]{:S(2)}, u32[]{:S(2)}) collective-permute-start(bf16[192,768]{1,0:T(8,128)(2,1)} %param.20), channel_id=1, source_target_pairs={{0,2},{1,3},{2,0},{3,1},{4,6},{5,7},{6,4},{7,5},{8,10},{9,11},{10,... | collective-permute-start | bytes 884744 | tf_op jit(solution)/shard_map/ppermute | solution.py:294
  3.7 54.2 %collective-permute-start.7 = (bf16[192,768]{1,0:T(8,128)(2,1)}, bf16[192,768]{1,0:T(8,128)(2,1)}, u32[]{:S(2)}, u32[]{:S(2)}) collective-permute-start(bf16[192,768]{1,0:T(8,128)(2,1)} %param.20), channel_id=1, source_target_pairs={{0,1},{1,0},{2,3},{3,2},{4,5},{5,4},{6,7},{7,6},{8,9},{9,8},{10,11... | collective-permute-start | bytes 884744 | tf_op jit(solution)/shard_map/ppermute | solution.py:294
  5.2 28.1 %collective-permute-start = (bf16[1,672]{1,0:T(2,128)(2,1)S(1)}, bf16[1,672]{1,0:T(2,128)(2,1)S(1)}, u32[]{:S(2)}, u32[]{:S(2)}) collective-permute-start(bf16[1,672]{1,0:T(2,128)(2,1)S(1)} %reshape.175), channel_id=1, source_target_pairs={{0,2},{1,3},{2,0},{3,1},{4,6},{5,7},{6,4},{7,5},{8,10},{9,11},{10,... | collective-permute-start | bytes 4040 | tf_op jit(solution)/shard_map/ppermute | solution.py:294
  5.4 28.1 %collective-permute-start.1 = (bf16[1,672]{1,0:T(2,128)(2,1)S(1)}, bf16[1,672]{1,0:T(2,128)(2,1)S(1)}, u32[]{:S(2)}, u32[]{:S(2)}) collective-permute-start(bf16[1,672]{1,0:T(2,128)(2,1)S(1)} %reshape.175), channel_id=1, source_target_pairs={{0,1},{1,0},{2,3},{3,2},{4,5},{5,4},{6,7},{7,6},{8,9},{9,8},{10,11... | collective-permute-start | bytes 4040 | tf_op jit(solution)/shard_map/ppermute | solution.py:294
  5.9 53.4 %collective-permute-start.9 = (bf16[192,768]{1,0:T(8,128)(2,1)}, bf16[192,768]{1,0:T(8,128)(2,1)}, u32[]{:S(2)}, u32[]{:S(2)}) collective-permute-start(bf16[192,768]{1,0:T(8,128)(2,1)} %param.21), channel_id=1, source_target_pairs={{0,2},{1,3},{2,0},{3,1},{4,6},{5,7},{6,4},{7,5},{8,10},{9,11},{10,... | collective-permute-start | bytes 884744 | tf_op jit(solution)/shard_map/ppermute | solution.py:294
  33.5 27.1 %collective-permute-start.10 = (bf16[192,768]{1,0:T(8,128)(2,1)S(1)}, bf16[192,768]{1,0:T(8,128)(2,1)}, u32[]{:S(2)}, u32[]{:S(2)}) collective-permute-start(bf16[192,768]{1,0:T(8,128)(2,1)S(1)} %copy-done.25), channel_id=1, source_target_pairs={{0,1},{1,0},{2,3},{3,2},{4,5},{5,4},{6,7},{7,6},{8,9},{9,8},{10,11... | collective-permute-start | bytes 884744 | tf_op jit(solution)/shard_map/ppermute | solution.py:294
  34.5 18.2 %collective-permute-start.21 = (bf16[192,128]{1,0:T(8,128)(2,1)S(1)}, bf16[192,128]{1,0:T(8,128)(2,1)S(1)}, u32[]{:S(2)}, u32[]{:S(2)}) collective-permute-start(bf16[192,128]{1,0:T(8,128)(2,1)S(1)} %copy-done.33), channel_id=1, source_target_pairs={{0,2},{1,3},{2,0},{3,1},{4,6},{5,7},{6,4},{7,5},{8,10},{9,11},{10,... | collective-permute-start | bytes 147464 | tf_op jit(solution)/shard_map/ppermute | solution.py:294
  60.6 105.1 %collective-permute-start.15 = (bf16[192,3072]{1,0:T(8,128)(2,1)}, bf16[192,3072]{1,0:T(8,128)(2,1)}, u32[]{:S(2)}, u32[]{:S(2)}) collective-permute-start(bf16[192,3072]{1,0:T(8,128)(2,1)} %param.24), channel_id=1, source_target_pairs={{0,2},{1,3},{2,0},{3,1},{4,6},{5,7},{6,4},{7,5},{8,10},{9,11},{10,... | collective-permute-start | bytes 3538952 | tf_op jit(solution)/shard_map/ppermute | solution.py:294
  65.2 115.8 %collective-permute-start.16 = (bf16[192,3072]{1,0:T(8,128)(2,1)}, bf16[192,3072]{1,0:T(8,128)(2,1)}, u32[]{:S(2)}, u32[]{:S(2)}) collective-permute-start(bf16[192,3072]{1,0:T(8,128)(2,1)} %param.24), channel_id=1, source_target_pairs={{0,1},{1,0},{2,3},{3,2},{4,5},{5,4},{6,7},{7,6},{8,9},{9,8},{10,11... | collective-permute-start | bytes 3538952 | tf_op jit(solution)/shard_map/ppermute | solution.py:294
  71.6 102.3 %collective-permute-start.18 = (bf16[768,768]{1,0:T(8,128)(2,1)}, bf16[768,768]{1,0:T(8,128)(2,1)}, u32[]{:S(2)}, u32[]{:S(2)}) collective-permute-start(bf16[768,768]{1,0:T(8,128)(2,1)} %param.25), channel_id=1, source_target_pairs={{0,2},{1,3},{2,0},{3,1},{4,6},{5,7},{6,4},{7,5},{8,10},{9,11},{10,... | collective-permute-start | bytes 3538952 | tf_op jit(solution)/shard_map/ppermute | solution.py:294
  75.0 101.2 %collective-permute-start.19 = (bf16[768,768]{1,0:T(8,128)(2,1)}, bf16[768,768]{1,0:T(8,128)(2,1)}, u32[]{:S(2)}, u32[]{:S(2)}) collective-permute-start(bf16[768,768]{1,0:T(8,128)(2,1)} %param.25), channel_id=1, source_target_pairs={{0,1},{1,0},{2,3},{3,2},{4,5},{5,4},{6,7},{7,6},{8,9},{9,8},{10,11... | collective-permute-start | bytes 3538952 | tf_op jit(solution)/shard_map/ppermute | solution.py:294
  84.5 66.5 %collective-permute-start.14 = (bf16[192,768]{1,0:T(8,128)(2,1)}, bf16[192,768]{1,0:T(8,128)(2,1)S(1)}, u32[]{:S(2)}, u32[]{:S(2)}) collective-permute-start(bf16[192,768]{1,0:T(8,128)(2,1)} %collective-permute-done.12), channel_id=1, source_target_pairs={{0,1},{1,0},{2,3},{3,2},{4,5},{5,4},{6,7},{7,6},{8,9},{9,8},{10,11... | collective-permute-start | bytes 884744 | tf_op jit(solution)/shard_map/ppermute | solution.py:294
  173.9 77.1 %collective-permute-start.20 = (bf16[768,768]{1,0:T(8,128)(2,1)}, bf16[768,768]{1,0:T(8,128)(2,1)}, u32[]{:S(2)}, u32[]{:S(2)}) collective-permute-start(bf16[768,768]{1,0:T(8,128)(2,1)} %collective-permute-done.18), channel_id=1, source_target_pairs={{0,1},{1,0},{2,3},{3,2},{4,5},{5,4},{6,7},{7,6},{8,9},{9,8},{10,11... | collective-permute-start | bytes 3538952 | tf_op jit(solution)/shard_map/ppermute | solution.py:294
  438.3 54.6 %collective-permute-start.84 = (bf16[192,128]{1,0:T(8,128)(2,1)}, bf16[192,128]{1,0:T(8,128)(2,1)}, u32[]{:S(2)}, u32[]{:S(2)}) collective-permute-start(bf16[192,128]{1,0:T(8,128)(2,1)} %get-tuple-element.55), channel_id=1, source_target_pairs={{0,1},{1,0},{2,3},{3,2},{4,5},{5,4},{6,7},{7,6},{8,9},{9,8},{10,11... | collective-permute-start | bytes 147464 | tf_op jit(solution)/shard_map/ppermute | solution.py:294
  445.1 65.4 %collective-permute-start.83 = (bf16[192,128]{1,0:T(8,128)(2,1)}, bf16[192,128]{1,0:T(8,128)(2,1)S(1)}, u32[]{:S(2)}, u32[]{:S(2)}) collective-permute-start(bf16[192,128]{1,0:T(8,128)(2,1)} %get-tuple-element.54), channel_id=1, source_target_pairs={{0,1},{1,0},{2,3},{3,2},{4,5},{5,4},{6,7},{7,6},{8,9},{9,8},{10,11... | collective-permute-start | bytes 147464 | tf_op jit(solution)/shard_map/ppermute | solution.py:294
  449.1 188.9 %collective-permute-start.75 = (bf16[768,768]{1,0:T(8,128)(2,1)}, bf16[768,768]{1,0:T(8,128)(2,1)}, u32[]{:S(2)}, u32[]{:S(2)}) collective-permute-start(bf16[768,768]{1,0:T(8,128)(2,1)} %get-tuple-element.41), channel_id=1, source_target_pairs={{0,1},{1,0},{2,3},{3,2},{4,5},{5,4},{6,7},{7,6},{8,9},{9,8},{10,11... | collective-permute-start | bytes 3538952 | tf_op jit(solution)/shard_map/ppermute | solution.py:294
  456.0 99.3 %collective-permute-start.57 = (bf16[192,768]{1,0:T(8,128)(2,1)}, bf16[192,768]{1,0:T(8,128)(2,1)}, u32[]{:S(2)}, u32[]{:S(2)}) collective-permute-start(bf16[192,768]{1,0:T(8,128)(2,1)} %get-tuple-element.47), channel_id=1, source_target_pairs={{0,1},{1,0},{2,3},{3,2},{4,5},{5,4},{6,7},{7,6},{8,9},{9,8},{10,11... | collective-permute-start | bytes 884744 | tf_op jit(solution)/shard_map/ppermute | solution.py:294
  456.0 105.9 %collective-permute-start.56 = (bf16[192,768]{1,0:T(8,128)(2,1)S(1)}, bf16[192,768]{1,0:T(8,128)(2,1)S(1)}, u32[]{:S(2)}, u32[]{:S(2)}) collective-permute-start(bf16[192,768]{1,0:T(8,128)(2,1)S(1)} %get-tuple-element.46), channel_id=1, source_target_pairs={{0,1},{1,0},{2,3},{3,2},{4,5},{5,4},{6,7},{7,6},{8,9},{9,8},{10,11... | collective-permute-start | bytes 884744 | tf_op jit(solution)/shard_map/ppermute | solution.py:294
  494.1 18.6 %collective-permute-start.85 = (bf16[192,128]{1,0:T(8,128)(2,1)S(1)}, bf16[192,128]{1,0:T(8,128)(2,1)S(1)}, u32[]{:S(2)}, u32[]{:S(2)}) collective-permute-start(bf16[192,128]{1,0:T(8,128)(2,1)S(1)} %add_convert_fusion.8), channel_id=1, source_target_pairs={{0,2},{1,3},{2,0},{3,1},{4,6},{5,7},{6,4},{7,5},{8,10},{9,11},{10,... | collective-permute-start | bytes 147464 | tf_op jit(solution)/shard_map/ppermute | solution.py:294
  510.5 19.1 %collective-permute-start.25 = (f32[21,128]{1,0:T(8,128)S(1)}, f32[21,128]{1,0:T(8,128)S(1)}, u32[]{:S(2)}, u32[]{:S(2)}) collective-permute-start(f32[21,128]{1,0:T(8,128)S(1)} %fusion.101), channel_id=1, source_target_pairs={{0,2},{1,3},{2,0},{3,1},{4,6},{5,7},{6,4},{7,5},{8,10},{9,11},{10,... | collective-permute-start | bytes 32264 | tf_op jit(solution)/shard_map/ppermute | solution.py:294
  512.8 18.9 %collective-permute-start.86 = (bf16[192,64]{1,0:T(8,128)(2,1)S(1)}, bf16[192,64]{1,0:T(8,128)(2,1)S(1)}, u32[]{:S(2)}, u32[]{:S(2)}) collective-permute-start(bf16[192,64]{1,0:T(8,128)(2,1)S(1)} %dynamic-slice_convert_fusion.26), channel_id=1, source_target_pairs={{0,4},{4,0},{8,12},{12,8},{16,20},{20,16},{24,28},{28,24},{1,5},{5... | collective-permute-start | bytes 73736 | tf_op jit(solution)/shard_map/ppermute | solution.py:294
  577.7 83.1 %collective-permute-start.74 = (bf16[768,768]{1,0:T(8,128)(2,1)S(1)}, bf16[768,768]{1,0:T(8,128)(2,1)S(1)}, u32[]{:S(2)}, u32[]{:S(2)}) collective-permute-start(bf16[768,768]{1,0:T(8,128)(2,1)S(1)} %copy-done.19), channel_id=1, source_target_pairs={{0,1},{1,0},{2,3},{3,2},{4,5},{5,4},{6,7},{7,6},{8,9},{9,8},{10,11... | collective-permute-start | bytes 3538952 | tf_op jit(solution)/shard_map/ppermute | solution.py:294
  580.9 62.4 %collective-permute-start.66 = (bf16[192,3072]{1,0:T(8,128)(2,1)S(1)}, bf16[192,3072]{1,0:T(8,128)(2,1)S(1)}, u32[]{:S(2)}, u32[]{:S(2)}) collective-permute-start(bf16[192,3072]{1,0:T(8,128)(2,1)S(1)} %copy-done.20), channel_id=1, source_target_pairs={{0,1},{1,0},{2,3},{3,2},{4,5},{5,4},{6,7},{7,6},{8,9},{9,8},{10,11... | collective-permute-start | bytes 3538952 | tf_op jit(solution)/shard_map/ppermute | solution.py:294
  582.0 92.5 %collective-permute-start.65 = (bf16[192,3072]{1,0:T(8,128)(2,1)S(1)}, bf16[192,3072]{1,0:T(8,128)(2,1)S(1)}, u32[]{:S(2)}, u32[]{:S(2)}) collective-permute-start(bf16[192,3072]{1,0:T(8,128)(2,1)S(1)} %copy-done.18), channel_id=1, source_target_pairs={{0,1},{1,0},{2,3},{3,2},{4,5},{5,4},{6,7},{7,6},{8,9},{9,8},{10,11... | collective-permute-start | bytes 3538952 | tf_op jit(solution)/shard_map/ppermute | solution.py:294
  643.2 27.8 %collective-permute-start.76 = (bf16[768,768]{1,0:T(8,128)(2,1)S(1)}, bf16[768,768]{1,0:T(8,128)(2,1)S(1)}, u32[]{:S(2)}, u32[]{:S(2)}) collective-permute-start(bf16[768,768]{1,0:T(8,128)(2,1)S(1)} %add_convert_fusion), channel_id=1, source_target_pairs={{0,2},{1,3},{2,0},{3,1},{4,6},{5,7},{6,4},{7,5},{8,10},{9,11},{10,... | collective-permute-start | bytes 3538952 | tf_op jit(solution)/shard_map/ppermute | solution.py:294
  644.5 39.2 %collective-permute-start.67 = (bf16[192,3072]{1,0:T(8,128)(2,1)S(1)}, bf16[192,3072]{1,0:T(8,128)(2,1)S(1)}, u32[]{:S(2)}, u32[]{:S(2)}) collective-permute-start(bf16[192,3072]{1,0:T(8,128)(2,1)S(1)} %add_convert_fusion.1), channel_id=1, source_target_pairs={{0,2},{1,3},{2,0},{3,1},{4,6},{5,7},{6,4},{7,5},{8,10},{9,11},{10,... | collective-permute-start | bytes 3538952 | tf_op jit(solution)/shard_map/ppermute | solution.py:294
  660.7 25.1 %collective-permute-start.35 = (bf16[48,384]{1,0:T(8,128)(2,1)S(1)}, bf16[48,384]{1,0:T(8,128)(2,1)S(1)}, u32[]{:S(2)}, u32[]{:S(2)}) collective-permute-start(bf16[48,384]{1,0:T(8,128)(2,1)S(1)} %add_convert_fusion.12), channel_id=1, source_target_pairs={{0,16},{4,20},{8,24},{12,28},{16,0},{20,4},{24,8},{28,12},{1,17},{... | collective-permute-start | bytes 110600 | tf_op jit(solution)/shard_map/ppermute | solution.py:294
  660.8 25.6 %collective-permute-start.63 = (bf16[96,384]{1,0:T(8,128)(2,1)S(1)}, bf16[96,384]{1,0:T(8,128)(2,1)S(1)}, u32[]{:S(2)}, u32[]{:S(2)}) collective-permute-start(bf16[96,384]{1,0:T(8,128)(2,1)S(1)} %maximum_select_fusion.17), channel_id=1, source_target_pairs={{0,8},{4,12},{8,0},{12,4},{16,24},{20,28},{24,16},{28,20},{1,9},{5... | collective-permute-start | bytes 221192 | tf_op jit(solution)/shard_map/ppermute | solution.py:294
  671.1 60.0 %collective-permute-start.54 = (bf16[96,384]{1,0:T(8,128)(2,1)S(1)}, bf16[96,384]{1,0:T(8,128)(2,1)S(1)}, u32[]{:S(2)}, u32[]{:S(2)}) collective-permute-start(bf16[96,384]{1,0:T(8,128)(2,1)S(1)} %maximum_select_fusion.16), channel_id=1, source_target_pairs={{0,8},{4,12},{8,0},{12,4},{16,24},{20,28},{24,16},{28,20},{1,9},{5... | collective-permute-start | bytes 221192 | tf_op jit(solution)/shard_map/ppermute | solution.py:294
  674.5 66.7 %collective-permute-start.45 = (bf16[96,384]{1,0:T(8,128)(2,1)S(1)}, bf16[96,384]{1,0:T(8,128)(2,1)S(1)}, u32[]{:S(2)}, u32[]{:S(2)}) collective-permute-start(bf16[96,384]{1,0:T(8,128)(2,1)S(1)} %maximum_select_fusion.15), channel_id=1, source_target_pairs={{0,8},{4,12},{8,0},{12,4},{16,24},{20,28},{24,16},{28,20},{1,9},{5... | collective-permute-start | bytes 221192 | tf_op jit(solution)/shard_map/ppermute | solution.py:294
  686.4 54.9 %collective-permute-start.36 = (bf16[96,384]{1,0:T(8,128)(2,1)S(1)}, bf16[96,384]{1,0:T(8,128)(2,1)S(1)}, u32[]{:S(2)}, u32[]{:S(2)}) collective-permute-start(bf16[96,384]{1,0:T(8,128)(2,1)S(1)} %maximum_select_fusion.14), channel_id=1, source_target_pairs={{0,8},{4,12},{8,0},{12,4},{16,24},{20,28},{24,16},{28,20},{1,9},{5... | collective-permute-start | bytes 221192 | tf_op jit(solution)/shard_map/ppermute | solution.py:294
  693.6 56.9 %collective-permute-start.64 = (bf16[192,384]{1,0:T(8,128)(2,1)S(1)}, bf16[192,384]{1,0:T(8,128)(2,1)S(1)}, u32[]{:S(2)}, u32[]{:S(2)}) collective-permute-start(bf16[192,384]{1,0:T(8,128)(2,1)S(1)} %maximum_select_fusion.13), channel_id=1, source_target_pairs={{0,4},{4,0},{8,12},{12,8},{16,20},{20,16},{24,28},{28,24},{1,5},{5... | collective-permute-start | bytes 442376 | tf_op jit(solution)/shard_map/ppermute | solution.py:294
  (107 other events, 1612.5 us)
